TPU v7x, 512 devices: a whole 4x4x16 slice. The times are simulated.
512 devices in a mesh: space: 128 (over z, y, core), tm: 4 (over x).
Axes of the slice: x: 4, y: 4, z: 16, core: 2. Of those that a mesh axis runs over, the one named last changes fastest.
Arguments:
- snapshots: bfloat16 [262144, 2048], P('space', 'tm'), as said below
- sketch: bfloat16 [2048, 256], P('tm'), may hold values from -0.125 to 0.125
- rotation: float32 [256, 256], replicated, may hold values from -0.375 to 0.375
Outputs:
- basis: float32 [262144, 256], P(('space', 'tm'))
- triangle: float32 [256, 256], replicated
Inputs may be any that keep to these rules, and one draw needn't show every extreme that they name: `snapshots`: the sketch has full column rank.
All inputs are finite; a program needn't handle non-finite values.
Results may differ from a plain program's by a relative error of at most 0.0003.
Values sent between devices are 32-bit elements; how exact they have to be, the bound alone decides.
A program may use at most 64 MiB of HBM per device.

v0:
```python
import jax
import jax.numpy as jnp
from jax import lax
from jax.sharding import PartitionSpec as P


def shards(snapshots, sketch, rotation):
    sketched = lax.psum_scatter(
        jnp.dot(snapshots, sketch, preferred_element_type=jnp.float32),
        "tm",
        scatter_dimension=0,
        tiled=True,
    )
    gram = lax.dot_general(
        sketched,
        sketched,
        (((0,), (0,)), ((), ())),
        precision=lax.Precision.HIGHEST,
        preferred_element_type=jnp.float32,
    )
    gram = lax.psum(gram, ("space", "tm"))
    lower = jnp.linalg.cholesky(gram)
    orthonormal = lax.linalg.triangular_solve(
        lower, sketched, left_side=False, lower=True, transpose_a=True
    )
    cell_count = sketched.shape[0] * lax.axis_size("space") * lax.axis_size("tm")
    scale = jnp.sqrt(jnp.float32(cell_count))
    basis = scale * jnp.dot(
        orthonormal, rotation, precision=lax.Precision.HIGHEST, preferred_element_type=jnp.float32
    )
    triangle = lower.T / scale
    return (basis, triangle)


def solution(mesh):
    in_specs = (P("space", "tm"), P("tm", None), P())
    out_specs = (P(("space", "tm"), None), P())
    return jax.shard_map(shards, mesh=mesh, in_specs=in_specs, out_specs=out_specs, check_vma=False)
```

profile of v0, /device:TPU:4, one launch (start us, length us, event | category | flops | bytes accessed | tf_op | source)
XLA Modules:
  0.0 592.6 jit_solution(8189028408867632442)
XLA Ops:
  7.2 0.0 copy-start
  7.2 0.0 reduce-scatter.2.cloned.1.call-start
  7.2 1.5 copy-done
  8.8 3.0 fusion.14
  11.8 0.0 reduce-scatter.2.cloned.1.call-update
  11.8 0.0 all-reduce.3.cloned.1.call-start
  11.8 40.3 %reduce-scatter.2.cloned.1.call-done = f32[512,256]{1,0:T(8,128)} async-done(((f32[2048,256]{1,0:T(8,128)}), f32[512,256]{1,0:T(8,128)}) %reduce-scatter.2.cloned.1.call-update) | async-done | bytes 524304 | tf_op jit(solution)/shard_map/reduce_scatter | solution.py:8
  52.2 2.9 fusion.15
  55.1 0.0 all-reduce.3.cloned.1.call-update
  55.1 0.0 copy-start.1
  55.1 462.1 %all-reduce.3.cloned.1.call-done = f32[256,256]{0,1:T(8,128)} async-done(((f32[256,256]{0,1:T(8,128)}), f32[256,256]{0,1:T(8,128)}) %all-reduce.3.cloned.1.call-update) | async-done | bytes 262160 | tf_op jit(solution)/shard_map/psum | solution.py:21
  517.2 1.1 copy.6
  518.3 1.0 fusion.5
  519.3 11.7 %cholesky.50 = f32[128,128]{1,0:T(8,128)S(1)} custom-call(f32[128,128]{1,0:T(8,128)S(1)} %cholesky.118), custom_call_target="Cholesky" | custom-call | tf_op jit(solution)/shard_map/jit(cholesky)/cholesky | solution.py:22
  531.1 9.8 %custom-call.14 = f32[1,128,128]{1,2,0:T(8,128)S(1)} custom-call(f32[1,128,128]{2,1,0:T(8,128)S(1)} %get-tuple-element.27), custom_call_target="InvertDiagBlocksLowerTriangular" | custom-call | tf_op jit(solution)/shard_map/jit(cholesky)/cholesky | solution.py:22
  540.9 0.2 constant_dynamic-update-slice_fusion.1
  541.1 0.3 convolution_subtract_fusion.1
  541.4 11.7 %cholesky.105 = f32[128,128]{1,0:T(8,128)S(1)} custom-call(f32[128,128]{1,0:T(8,128)S(1)} %convolution_subtract_fusion.1), custom_call_target="Cholesky" | custom-call | tf_op jit(solution)/shard_map/jit(cholesky)/cholesky | solution.py:22
  553.2 0.7 compare_reduce_fusion
  555.3 0.1 triangular_solve.58
  555.3 4.2 while.1
  555.5 0.6 fusion.26
  556.1 1.4 bitcast_dynamic-update-slice_fusion.2
  557.6 0.6 fusion.26
  558.1 1.4 bitcast_dynamic-update-slice_fusion.2
  559.6 0.0 copy-start.2
  559.6 0.6 copy-done.2
  560.2 20.5 %custom-call.15 = f32[2,128,128]{1,2,0:T(8,128)S(1)} custom-call(f32[2,128,128]{2,1,0:T(8,128)} %copy-done.2), custom_call_target="InvertDiagBlocksLowerTriangular" | custom-call | tf_op jit(solution)/shard_map/triangular_solve | solution.py:23
  580.7 0.0 copy-done.1
  580.7 0.4 fusion.3
  581.2 0.6 convolution_subtract_fusion
  581.8 0.4 fusion.7
  582.2 0.8 copy.7
  583.0 2.7 convolution_multiply_fusion
  (9 shorter events, 0.2 us)
Async XLA Ops:
  7.2 1.6 copy-start
  7.2 45.0 %reduce-scatter.2.cloned.1.call-start = ((), (), s32[]{:S(2)}) async-start(), calls=%async_computation.1 | async-start | bytes 2621440 | tf_op jit(solution)/shard_map/reduce_scatter | solution.py:8
  11.8 505.5 %all-reduce.3.cloned.1.call-start = ((), (), s32[]{:S(2)}) async-start(), calls=%async_computation.2 | async-start | bytes 524288 | tf_op jit(solution)/shard_map/psum | solution.py:21
  55.1 525.6 %copy-start.1 = (f32[512,256]{1,0:T(8,128)S(1)}, f32[512,256]{1,0:T(8,128)}, u32[]{:S(2)}) copy-start(f32[512,256]{1,0:T(8,128)} %reduce-scatter.2.cloned.1.call-done) | copy-start | bytes 1572868
  559.6 0.7 copy-start.2
Sparse Core Ops, SparseCore 0:
  11.9 40.2 reduce-scatter.1
  59.1 458.1 all-reduce.2
where the time goes:
time: 593 us
  waiting for transfers between devices  502 us (85%)
  other arithmetic  55.5 us (9%)
  between operations  15.5 us (3%)
  matrix products  10.5 us (2%)
  local copies, waits for them, and re-layouts  8.27 us (1%)
    psum x1, waiting for transfers between devices, shards(): gram = lax.psum(gram, ('space', 'tm'))  462 us
    reduce_scatter x1, waiting for transfers between devices, shards(): lax.psum_scatter(jnp.dot(snapshots, sketch, preferred_element_type=jnp.fl...  40.3 us
    another operation x6, other arithmetic, shards(): lower = jnp.linalg.cholesky(gram)  34 us
    another operation x2, other arithmetic, shards(): lax.linalg.triangular_solve(lower, sketched, left_side=False, lower=True,...  20.5 us
  transfers between devices with their start and end apart: 2, of which 2 were waited for; matrix products, arithmetic and copies ran while one was open for 0% of the time, Pallas kernels for 0%

commit v1 on v0

--- a/solution.py
+++ b/solution.py
@@ -18,7 +18,7 @@
         precision=lax.Precision.HIGHEST,
         preferred_element_type=jnp.float32,
     )
-    gram = lax.psum(gram, ("space", "tm"))
+    gram = lax.psum(lax.psum(gram, axis_name="space"), axis_name="tm")
     lower = jnp.linalg.cholesky(gram)
     orthonormal = lax.linalg.triangular_solve(
         lower, sketched, left_side=False, lower=True, transpose_a=True

time: 593 us -> 518 us (0.87)
  the two profiles are of different devices: /device:TPU:4 before, /device:TPU:8 now
where the time goes in v1:
time: 518 us
  waiting for transfers between devices  428 us (83%)
  other arithmetic  55.5 us (11%)
  between operations  15.2 us (3%)
  matrix products  10.5 us (2%)
  local copies, waits for them, and re-layouts  8.27 us (2%)
    psum x2, waiting for transfers between devices, shards(): gram = lax.psum(lax.psum(gram, axis_name='space'), axis_name='tm')  386 us
    reduce_scatter x1, waiting for transfers between devices, shards(): lax.psum_scatter(jnp.dot(snapshots, sketch, preferred_element_type=jnp.fl...  41.8 us
    another operation x6, other arithmetic, shards(): lower = jnp.linalg.cholesky(gram)  34 us
    another operation x2, other arithmetic, shards(): lax.linalg.triangular_solve(lower, sketched, left_side=False, lower=True,...  20.5 us
  transfers between devices with their start and end apart: 3, of which 3 were waited for; matrix products, arithmetic and copies ran while one was open for 0% of the time, Pallas kernels for 0%

profile of v1, /device:TPU:8, one launch (start us, length us, event | category | flops | bytes accessed | tf_op | source)
XLA Modules:
  0.0 517.6 jit_solution(1128079094507511957)
XLA Ops:
  7.2 0.0 copy-start
  7.2 0.0 reduce-scatter.2.cloned.1.call-start
  7.2 1.5 copy-done
  8.8 3.0 fusion.14
  11.8 0.0 reduce-scatter.2.cloned.1.call-update
  11.8 0.0 all-reduce.4.cloned.1.call-start
  11.8 41.8 %reduce-scatter.2.cloned.1.call-done = f32[512,256]{1,0:T(8,128)} async-done(((f32[2048,256]{1,0:T(8,128)}), f32[512,256]{1,0:T(8,128)}) %reduce-scatter.2.cloned.1.call-update) | async-done | bytes 524304 | tf_op jit(solution)/shard_map/reduce_scatter | solution.py:8
  53.6 2.9 fusion.15
  56.5 0.0 all-reduce.4.cloned.1.call-update
  56.6 0.0 all-reduce.6.cloned.1.call-start
  56.6 329.5 %all-reduce.4.cloned.1.call-done = f32[256,256]{0,1:T(8,128)} async-done(((f32[256,256]{0,1:T(8,128)}), f32[256,256]{0,1:T(8,128)}) %all-reduce.4.cloned.1.call-update) | async-done | bytes 262160 | tf_op jit(solution)/shard_map/psum | solution.py:21
  386.1 0.0 all-reduce.6.cloned.1.call-update
  386.2 0.0 copy-start.1
  386.2 56.4 %all-reduce.6.cloned.1.call-done = f32[256,256]{0,1:T(8,128)} async-done(((f32[256,256]{0,1:T(8,128)}), f32[256,256]{0,1:T(8,128)}) %all-reduce.6.cloned.1.call-update) | async-done | bytes 262160 | tf_op jit(solution)/shard_map/psum | solution.py:21
  442.6 1.1 copy.6
  443.7 1.0 fusion.5
  444.7 11.7 %cholesky.50 = f32[128,128]{1,0:T(8,128)S(1)} custom-call(f32[128,128]{1,0:T(8,128)S(1)} %cholesky.118), custom_call_target="Cholesky" | custom-call | tf_op jit(solution)/shard_map/jit(cholesky)/cholesky | solution.py:22
  456.4 9.8 %custom-call.14 = f32[1,128,128]{1,2,0:T(8,128)S(1)} custom-call(f32[1,128,128]{2,1,0:T(8,128)S(1)} %get-tuple-element.27), custom_call_target="InvertDiagBlocksLowerTriangular" | custom-call | tf_op jit(solution)/shard_map/jit(cholesky)/cholesky | solution.py:22
  466.3 0.2 constant_dynamic-update-slice_fusion.1
  466.5 0.3 convolution_subtract_fusion.1
  466.8 11.7 %cholesky.105 = f32[128,128]{1,0:T(8,128)S(1)} custom-call(f32[128,128]{1,0:T(8,128)S(1)} %convolution_subtract_fusion.1), custom_call_target="Cholesky" | custom-call | tf_op jit(solution)/shard_map/jit(cholesky)/cholesky | solution.py:22
  478.5 0.7 compare_reduce_fusion
  480.6 0.1 triangular_solve.58
  480.7 4.2 while.1
  480.9 0.6 fusion.26
  481.4 1.4 bitcast_dynamic-update-slice_fusion.2
  482.9 0.6 fusion.26
  483.5 1.4 bitcast_dynamic-update-slice_fusion.2
  484.9 0.0 copy-start.2
  485.0 0.6 copy-done.2
  485.6 20.5 %custom-call.15 = f32[2,128,128]{1,2,0:T(8,128)S(1)} custom-call(f32[2,128,128]{2,1,0:T(8,128)} %copy-done.2), custom_call_target="InvertDiagBlocksLowerTriangular" | custom-call | tf_op jit(solution)/shard_map/triangular_solve | solution.py:23
  506.1 0.0 copy-done.1
  506.1 0.4 fusion.3
  506.5 0.6 convolution_subtract_fusion
  507.1 0.4 fusion.7
  507.5 0.8 copy.7
  508.4 2.7 convolution_multiply_fusion
  (9 shorter events, 0.2 us)
Async XLA Ops:
  7.2 1.6 copy-start
  7.2 46.5 %reduce-scatter.2.cloned.1.call-start = ((), (), s32[]{:S(2)}) async-start(), calls=%async_computation.1 | async-start | bytes 2621440 | tf_op jit(solution)/shard_map/reduce_scatter | solution.py:8
  11.8 374.3 %all-reduce.4.cloned.1.call-start = ((), (), s32[]{:S(2)}) async-start(), calls=%async_computation.2 | async-start | bytes 524288 | tf_op jit(solution)/shard_map/psum | solution.py:21
  56.6 386.0 %all-reduce.6.cloned.1.call-start = ((), (), s32[]{:S(2)}) async-start(), calls=%async_computation.3 | async-start | bytes 524288 | tf_op jit(solution)/shard_map/psum | solution.py:21
  386.2 119.9 %copy-start.1 = (f32[512,256]{1,0:T(8,128)S(1)}, f32[512,256]{1,0:T(8,128)}, u32[]{:S(2)}) copy-start(f32[512,256]{1,0:T(8,128)} %reduce-scatter.2.cloned.1.call-done) | copy-start | bytes 1572868
  484.9 0.7 copy-start.2
Sparse Core Ops, SparseCore 0:
  11.9 41.6 reduce-scatter.1
  58.1 328.0 all-reduce.3
  388.6 54.0 all-reduce.5
